TPU v7x, 128 devices: a whole 4x4x4 slice. The times are simulated.
128 devices in a mesh: tok: 16 (over z, y), mdl: 8 (over x, core).
Axes of the slice: x: 4, y: 4, z: 4, core: 2. Of those that a mesh axis runs over, the one named last changes fastest.
Arguments:
- tokens: bfloat16 [4096, 5120], P('tok'), may hold values from -32 to 32
- norm_gain: bfloat16 [5120], replicated, may hold values from 0.099609375 to 1.8984375
- w_query: bfloat16 [5120, 4096], P(None, 'mdl'), may hold values from -0.078125 to 0.078125
- w_key: bfloat16 [5120, 1024], P(None, 'mdl'), may hold values from -0.3125 to 0.3125
- w_value: bfloat16 [5120, 1024], P(None, 'mdl'), may hold values from -0.078125 to 0.078125
- w_out: bfloat16 [4096, 5120], P('mdl'), may hold values from -0.09375 to 0.09375
- prompt_keys: bfloat16 [6, 4096, 8, 128], P(None, 'tok', 'mdl'), may hold values from -6 to 6
- prompt_values: bfloat16 [6, 4096, 8, 128], P(None, 'tok', 'mdl'), may hold values from -24 to 24
- cache_keys: bfloat16 [128, 2048, 8, 128], P('tok', None, 'mdl'), may hold values from -6 to 6
- cache_values: bfloat16 [128, 2048, 8, 128], P('tok', None, 'mdl'), may hold values from -24 to 24
- cache_length: int32 [128], P('tok'), may hold values from 1 to 2048, as said below
- request_group: int32 [128], replicated, may hold values from 0 to 5
- ancestors: int32 [128, 32, 32], P('tok'), may hold values from 0 to 1, as said below
- accepted: int32 [128, 8], P('tok'), may hold values from -1 to 31, as said below
Outputs:
- attention_out: bfloat16 [4096, 5120], P('tok', 'mdl')
- compact_rows: bfloat16 [128, 8, 5120], P('tok', None, 'mdl')
Inputs may be any that keep to these rules, and one draw needn't show every extreme that they name: `cache_length`: some request has exactly 2048 live slots. ancestors[r, a, b] is 1 where tree slot b is slot a itself or an ancestor of it in request r's draft tree, else 0; each tree has one root, and slots are in no particular order. Entry k of request r is the tree slot of the accepted path's node at depth k, from the root on, for k below the path's length, and -1 after it; a path holds 1 to 8 nodes, and some request's path holds 8.
All inputs are finite; a program needn't handle non-finite values.
Results may differ from a plain program's by a relative error of at most 0.017.
Values may be sent and summed in bfloat16 or wider, within the bound.
No kernel may reach another device: no remote copies, remote signals or barrier semaphores. Data moves between devices by JAX's collectives and lax.ppermute only.
A program may use at most 128 MiB of HBM per device.

v0:
```python
import jax
import jax.numpy as jnp
from jax import lax
from jax.sharding import PartitionSpec as P

PROMPT = 4096
THETA = 100000000.0
EPS = 1e-05


def rotate_pairs(vectors, positions):
    middle = vectors.shape[-1] // 2
    exponent = jnp.arange(middle, dtype=jnp.float32) * (2.0 / vectors.shape[-1])
    inverse = jnp.power(jnp.float32(THETA), -exponent)
    angles = positions.astype(jnp.float32)[:, None] * inverse[None, :]
    cosine = jnp.cos(angles)[:, None, :]
    sine_part = jnp.sin(angles)[:, None, :]
    leading = vectors[..., :middle]
    trailing = vectors[..., middle:]
    return jnp.concatenate(
        [leading * cosine - trailing * sine_part, trailing * cosine + leading * sine_part], axis=-1
    )


def slice_attention(grouped, chosen_keys, chosen_values, slice_rows, factor):
    pieces = chosen_keys.shape[1] // slice_rows
    layout = (chosen_keys.shape[0], pieces, slice_rows, chosen_keys.shape[2], chosen_keys.shape[3])
    keys_split = chosen_keys.reshape(layout)
    values_split = chosen_values.reshape(layout)
    scores = (
        jnp.einsum("ntkgd,nsckd->ntkgsc", grouped, keys_split, preferred_element_type=jnp.float32)
        * factor
    )
    weights = jnp.exp(scores)
    totals = jnp.sum(weights, axis=5)
    numerator = jnp.einsum(
        "ntkgsc,nsckd->ntkgsd",
        weights.astype(jnp.bfloat16),
        values_split,
        preferred_element_type=jnp.float32,
    )
    outputs = (numerator / totals[..., None]).astype(jnp.bfloat16)
    return (outputs, totals)


def cache_block(grouped, key_block, value_block, lengths, factor):
    scores = (
        jnp.einsum("ntkgd,nckd->ntkgc", grouped, key_block, preferred_element_type=jnp.float32)
        * factor
    )
    places = jnp.arange(key_block.shape[1], dtype=jnp.int32)
    live = places[None, :] < lengths[:, None]
    weights = jnp.where(live[:, None, None, None, :], jnp.exp(scores), 0.0)
    numerator = jnp.einsum(
        "ntkgc,nckd->ntkgd",
        weights.astype(jnp.bfloat16),
        value_block,
        preferred_element_type=jnp.float32,
    )
    return (numerator, jnp.sum(weights, axis=4))


def shards(
    tokens,
    norm_gain,
    w_query,
    w_key,
    w_value,
    w_out,
    prompt_keys,
    prompt_values,
    cache_keys,
    cache_values,
    cache_length,
    request_group,
    ancestors,
    accepted,
):
    requests = cache_length.shape[0]
    tree_size = ancestors.shape[1]
    head_dim = prompt_keys.shape[3]
    key_heads = prompt_keys.shape[2]
    query_heads = w_query.shape[1] // head_dim
    group_size = query_heads // key_heads
    slice_rows = prompt_keys.shape[1]
    factor = head_dim ** (-0.5)
    rows_local = tokens.shape[0]
    wide = tokens.astype(jnp.float32)
    normed = (
        wide
        * lax.rsqrt(jnp.mean(wide * wide, axis=1, keepdims=True) + EPS)
        * norm_gain.astype(jnp.float32)
    ).astype(jnp.bfloat16)
    queries = jnp.dot(normed, w_query, preferred_element_type=jnp.float32).reshape(
        rows_local, query_heads, head_dim
    )
    new_keys = jnp.dot(normed, w_key, preferred_element_type=jnp.float32).reshape(
        rows_local, key_heads, head_dim
    )
    new_values = (
        jnp.dot(normed, w_value, preferred_element_type=jnp.float32)
        .astype(jnp.bfloat16)
        .reshape(requests, tree_size, key_heads, head_dim)
    )
    depth = jnp.sum(ancestors, axis=2) - 1
    positions = (PROMPT + cache_length[:, None] + depth).reshape(rows_local)
    queries = rotate_pairs(queries, positions).astype(jnp.bfloat16)
    new_keys = (
        rotate_pairs(new_keys, positions)
        .astype(jnp.bfloat16)
        .reshape(requests, tree_size, key_heads, head_dim)
    )
    grouped = queries.reshape(requests, tree_size, key_heads, group_size, head_dim)
    first_request = lax.axis_index("tok") * requests
    own_groups = lax.dynamic_slice_in_dim(request_group, first_request, requests)
    chosen_keys = jnp.take(
        lax.all_gather(prompt_keys, "tok", axis=1, tiled=True), own_groups, axis=0
    )
    chosen_values = jnp.take(
        lax.all_gather(prompt_values, "tok", axis=1, tiled=True), own_groups, axis=0
    )
    outputs, totals = slice_attention(grouped, chosen_keys, chosen_values, slice_rows, factor)
    weighted = jnp.sum(totals[..., None] * outputs.astype(jnp.float32), axis=4)
    prompt_total = jnp.sum(totals, axis=4)
    cache_part, cache_total = cache_block(grouped, cache_keys, cache_values, cache_length, factor)
    tree_scores = (
        jnp.einsum("ntkgd,nmkd->ntkgm", grouped, new_keys, preferred_element_type=jnp.float32)
        * factor
    )
    tree_weights = jnp.where(ancestors[:, :, None, None, :] > 0, jnp.exp(tree_scores), 0.0)
    tree_part = jnp.einsum(
        "ntkgm,nmkd->ntkgd",
        tree_weights.astype(jnp.bfloat16),
        new_values,
        preferred_element_type=jnp.float32,
    )
    denominator = prompt_total + cache_total + jnp.sum(tree_weights, axis=4)
    merged = (weighted + cache_part + tree_part) / denominator[..., None]
    attended = merged.astype(jnp.bfloat16).reshape(rows_local, query_heads * head_dim)
    projected = jnp.dot(attended, w_out, preferred_element_type=jnp.float32)
    attention_out = lax.psum_scatter(
        projected.astype(jnp.bfloat16), "mdl", scatter_dimension=1, tiled=True
    )
    columns = attention_out.shape[1]
    column_start = lax.axis_index("mdl") * columns
    residual = lax.dynamic_slice_in_dim(tokens, column_start, columns, 1).astype(
        jnp.float32
    ) + attention_out.astype(jnp.float32)
    rows_index = (
        jnp.arange(requests, dtype=jnp.int32)[:, None] * tree_size + jnp.maximum(accepted, 0)
    ).reshape(requests * accepted.shape[1])
    picked = jnp.take(residual, rows_index, axis=0).reshape(requests, accepted.shape[1], columns)
    compact_rows = jnp.where(accepted[:, :, None] >= 0, picked, 0.0).astype(jnp.bfloat16)
    return (attention_out, compact_rows)


def solution(mesh):
    placed = (
        P("tok", None),
        P(),
        P(None, "mdl"),
        P(None, "mdl"),
        P(None, "mdl"),
        P("mdl", None),
        P(None, "tok", "mdl", None),
        P(None, "tok", "mdl", None),
        P("tok", None, "mdl", None),
        P("tok", None, "mdl", None),
        P("tok"),
        P(),
        P("tok", None, None),
        P("tok", None),
    )
    return jax.shard_map(
        shards,
        mesh=mesh,
        in_specs=placed,
        out_specs=(P("tok", "mdl"), P("tok", None, "mdl")),
        check_vma=False,
    )
```

profile of v0, /device:TPU:0, one launch (start us, length us, event | category | flops | bytes accessed | tf_op | source)
XLA Modules:
  0.0 233.8 jit_solution(10917397976916189196)
XLA Ops:
  7.2 0.0 copy-start
  7.2 0.0 all-gather.3.cloned.1.call-start
  7.2 0.7 all-gather.3.cloned.1.call-update
  7.9 0.0 all-gather.5.cloned.1.call-start
  8.0 0.7 all-gather.5.cloned.1.call-update
  8.7 0.0 reduce-scatter.4.cloned.1.call-start
  8.7 0.7 convert_element_type.64
  9.4 2.3 %fusion.8 = f32[256]{0:T(256)S(1)} fusion(bf16[256,5120]{1,0:T(8,128)(2,1)} %param.16), kind=kLoop, calls=%fused_computation.22 | loop fusion | flops 3931904 | bytes 2622464 | tf_op jit(solution)/shard_map/reduce_sum | solution.py:91
  11.8 0.0 copy-start.4
  11.8 0.0 copy-start.6
  11.8 4.9 %fusion.66 = f32[256,512]{1,0:T(8,128)S(1)} fusion(bf16[5120,512]{1,0:T(8,128)(2,1)} %param.18, bf16[256,5120]{1,0:T(8,128)(2,1)} %param.16, f32[5120]{0:T(1024)S(1)} %convert_element_type.64, f32[256]{0:T(256)S(1)} %add_rsqrt_fusion), kind=kOutput, calls=%fused_computation.98 | convolution fusion | flops 1347420160 | bytes 8410112 | tf_op jit(solution)/shard_map/dot_general | solution.py:94
  16.7 0.0 copy-start.7
  16.7 0.2 reshape.339
  16.9 0.0 copy-done.4
  16.9 0.2 reduce_sum.66
  17.1 0.0 copy-done.6
  17.1 0.1 add_convert_fusion.1
  17.2 0.1 convert_element_type.67
  17.3 0.0 copy-done
  17.3 2.9 %convolution_bitcast_fusion.1 = f32[256,1,128]{0,2,1:T(8,128)S(1)} fusion(bf16[5120,128]{1,0:T(8,128)(2,1)S(1)} %copy-done, bf16[256,5120]{1,0:T(8,128)(2,1)} %param.16, f32[5120]{0:T(1024)S(1)} %convert_element_type.64, f32[256]{0:T(256)S(1)} %add_rsqrt_fusion), kind=kOutput, calls=%fused_computation.43 | convolution fusion | flops 340787200 | bytes 4084736 | tf_op jit(solution)/shard_map/dot_general | solution.py:97
  20.2 0.3 fusion.54
  20.5 0.1 copy.34
  20.6 0.1 copy.35
  20.8 0.1 copy.33
  20.9 0.0 copy-done.7
  20.9 0.1 compare_and_fusion.1
  21.0 0.5 multiply_cosine_fusion
  21.5 0.3 fusion.68
  21.9 0.0 copy-start.2
  21.9 0.1 subtract_convert_fusion
  22.0 0.1 pad_maximum_fusion
  22.2 0.6 fusion.69
  22.8 3.7 %convolution_convert_fusion.1 = bf16[256,128]{1,0:T(8,128)(2,1)S(1)} fusion(bf16[5120,128]{1,0:T(8,128)(2,1)} %param.20, bf16[256,5120]{1,0:T(8,128)(2,1)} %param.16, f32[5120]{0:T(1024)S(1)} %convert_element_type.64, f32[256]{0:T(256)S(1)} %add_rsqrt_fusion), kind=kOutput, calls=%fused_computation.44 | convolution fusion | flops 340819968 | bytes 4019200 | tf_op jit(solution)/shard_map/dot_general | solution.py:101
  26.5 0.1 iota_compare_fusion
  26.6 0.0 copy-done.2
  26.6 5.2 %fusion.6 = (f32[8,32,4]{1,2,0:T(4,128)S(1)}, f32[8,32,4,2048]{3,1,2,0:T(8,128)}) fusion(pred[8,2048]{1,0:T(8,128)(4,1)S(1)} %iota_compare_fusion, bf16[8,2048,1,128]{3,1,2,0:T(8,128)(2,1)S(1)} %copy-done.2, bf16[8,32,4,128]{3,1,0,2:T(8,128)(2,1)S(1)} %pad_maximum_fusion), kind=kOutput, calls=%fused_computation.17 | convolution fusion | flops 543161344 | bytes 12865536 | tf_op jit(solution)/shard_map/ntkgd,nckd->ntkgc/dot_general | solution.py:48
  31.8 42.3 %all-gather.3.cloned.1.call-done = bf16[6,4096,1,128]{3,1,2,0:T(8,128)(2,1)} async-done(((bf16[6,256,1,128]{3,1,2,0:T(8,128)(2,1)}), bf16[6,4096,1,128]{3,1,2,0:T(8,128)(2,1)}) %all-gather.3.cloned.1.call-update) | async-done | bytes 6291472 | tf_op jit(solution)/shard_map/all_gather | solution.py:117
  74.1 7.6 %gather_fusion.1 = bf16[8,4096,128]{2,1,0:T(8,128)(2,1)} fusion(bf16[6,4096,128]{2,1,0:T(8,128)(2,1)} %bitcast.177, s32[1024]{0:T(1024)S(1)} %pad_clamp_fusion.1), kind=kCustom, calls=%fused_computation.clone | custom fusion | bytes 16777248 | tf_op jit(solution)/shard_map/jit(_take)/gather | solution.py:116
  81.7 55.5 %all-gather.5.cloned.1.call-done = bf16[6,4096,1,128]{3,1,2,0:T(8,128)(2,1)} async-done(((bf16[6,256,1,128]{3,1,2,0:T(8,128)(2,1)}), bf16[6,4096,1,128]{3,1,2,0:T(8,128)(2,1)}) %all-gather.5.cloned.1.call-update) | async-done | bytes 6291472 | tf_op jit(solution)/shard_map/all_gather | solution.py:120
  137.2 7.4 %gather_fusion.2 = bf16[8,4096,128]{2,1,0:T(8,128)(2,1)} fusion(bf16[6,4096,128]{2,1,0:T(8,128)(2,1)} %bitcast.178, s32[1024]{0:T(1024)S(1)} %pad_clamp_fusion.1), kind=kCustom, calls=%fused_computation.1.clone | custom fusion | bytes 16777248 | tf_op jit(solution)/shard_map/jit(_take)/gather | solution.py:119
  144.7 9.4 %bitcast_select_fusion.1 = (bf16[8,4096,1,128]{3,1,0,2:T(8,128)(2,1)}, bf16[8,4096,1,128]{3,1,0,2:T(8,128)(2,1)S(1)}) fusion(bf16[8,4096,128]{2,1,0:T(8,128)(2,1)} %gather_fusion.2, pred[8]{0:T(512)(128)(4,1)S(1)} %get-tuple-element.7, bf16[8,4096,128]{2,1,0:T(8,128)(2,1)} %gather_fusion.1), kind=kLoop, calls=%fused_computation.13 | loop fusion | flops 8388608 | bytes 33554440 | tf_op jit(solution)/shard_map/jit(_take)/select_n | solution.py:119
  154.1 7.9 %bitcast_reduce_fusion = (f32[8,32,4]{1,2,0:T(4,128)S(1)}, f32[8,32,4,16]{1,2,3,0:T(4,128)S(1)}, f32[8,16,256,32,4]{2,3,4,1,0:T(8,128)}) fusion(bf16[8,16,256,128,1]{3,2,4,1,0:T(8,128)(2,1)S(1)} %bitcast.176, bf16[8,32,4,128]{3,1,0,2:T(8,128)(2,1)S(1)} %pad_maximum_fusion), kind=kOutput, calls=%fused_computation.3 | convolution fusion | flops 1086307328 | bytes 25497600 | tf_op jit(solution)/shard_map/ntkgd,nsckd->ntkgsc/dot_general | solution.py:31
  162.0 10.1 %multiply_reduce_fusion = f32[8,32,4,128]{3,1,2,0:T(8,128)S(1)} fusion(f32[8,32,4,16]{1,2,3,0:T(4,128)S(1)} %get-tuple-element.4, bf16[8,16,256,128,1]{3,2,4,1,0:T(8,128)(2,1)} %bitcast.180, f32[8,16,256,32,4]{2,3,4,1,0:T(8,128)} %get-tuple-element.20), kind=kOutput, calls=%fused_computation.15 | convolution fusion | flops 1092485120 | bytes 25755648 | tf_op jit(solution)/shard_map/ntkgsc,nsckd->ntkgsd/dot_general | solution.py:36
  172.1 6.3 %fusion.31 = f32[8,32,1,4,128]{4,1,3,0,2:T(8,128)S(1)} fusion(bf16[8,2048,1,128]{3,1,2,0:T(8,128)(2,1)} %param.25, f32[8,32,4,2048]{3,1,2,0:T(8,128)} %get-tuple-element.24, pred[8,2048]{1,0:T(8,128)(4,1)S(1)} %iota_compare_fusion, f32[8,32,4,128]{3,1,2,0:T(8,128)S(1)} %multiply_reduce_fusion), kind=kOutput, calls=%fused_computation.40 | convolution fusion | flops 543293440 | bytes 13647872 | tf_op jit(solution)/shard_map/ntkgc,nckd->ntkgd/dot_general | solution.py:54
  178.4 0.3 fusion.36
  178.7 0.1 copy.37
  178.9 0.0 copy-start.1
  178.9 5.6 %convolution_convert_fusion = bf16[256,5120]{1,0:T(8,128)(2,1)} fusion(bf16[512,5120]{1,0:T(8,128)(2,1)} %param.21, bf16[32,8,4,128]{3,2,1,0:T(4,128)(2,1)S(1)} %bitcast.184), kind=kOutput, calls=%fused_computation.21 | convolution fusion | flops 1343488000 | bytes 8126464 | tf_op jit(solution)/shard_map/dot_general | solution.py:140
  184.5 0.0 copy-start.5
  184.5 4.4 %copy.47 = bf16[256,5120]{0,1:T(8,128)(2,1)} copy(bf16[256,5120]{1,0:T(8,128)(2,1)} %convolution_convert_fusion) | data formatting | bytes 5242880
  188.9 0.0 reduce-scatter.4.cloned.1.call-update
  188.9 0.0 copy-done.5
  188.9 0.1 compare_and_fusion
  189.0 0.1 reshape.349
  189.1 34.3 %reduce-scatter.4.cloned.1.call-done = bf16[640,256]{1,0:T(8,128)(2,1)} async-done(((bf16[5120,256]{1,0:T(8,128)(2,1)}), bf16[640,256]{1,0:T(8,128)(2,1)}) %reduce-scatter.4.cloned.1.call-update) | async-done | bytes 327696
  223.4 1.2 copy.48
  224.6 0.0 copy-start.3
  224.6 1.2 convert_add_fusion
  225.8 0.7 gather_fusion
  226.5 0.7 fusion.48
  227.2 0.0 copy-done.3
  227.2 0.0 copy-done.1
  (9 shorter events, 0.1 us)
Async XLA Ops:
  7.2 10.1 %copy-start = (bf16[5120,128]{1,0:T(8,128)(2,1)S(1)}, bf16[5120,128]{1,0:T(8,128)(2,1)}, u32[]{:S(2)}) copy-start(bf16[5120,128]{1,0:T(8,128)(2,1)} %param.19) | copy-start | bytes 3932164
  7.2 66.9 %all-gather.3.cloned.1.call-start = ((), (), s32[]{:S(2)}) async-start(), calls=%async_computation.1 | async-start | bytes 6684672 | tf_op jit(solution)/shard_map/all_gather | solution.py:117
  7.9 129.3 %all-gather.5.cloned.1.call-start = ((), (), s32[]{:S(2)}) async-start(), calls=%async_computation.2 | async-start | bytes 6684672 | tf_op jit(solution)/shard_map/all_gather | solution.py:120
  8.7 214.8 %reduce-scatter.4.cloned.1.call-start = ((), (), s32[]{:S(2)}) async-start(), calls=%async_computation.3 | async-start | bytes 2949120
  11.8 5.1 %copy-start.4 = (s32[8,32,32]{2,1,0:T(8,128)S(1)}, s32[8,32,32]{2,1,0:T(8,128)}, u32[]{:S(2)}) copy-start(s32[8,32,32]{2,1,0:T(8,128)} %param.28) | copy-start | bytes 98308
  11.8 5.3 %copy-start.6 = (s32[8]{0:T(128)S(1)}, s32[8]{0:T(128)}, u32[]{:S(2)}) copy-start(s32[8]{0:T(128)} %param.26) | copy-start | bytes 100
  16.7 4.2 %copy-start.7 = (s32[128]{0:T(128)S(1)}, s32[128]{0:T(128)}, u32[]{:S(2)}) copy-start(s32[128]{0:T(128)} %param.27) | copy-start | bytes 1540
  21.9 4.7 %copy-start.2 = (bf16[8,2048,1,128]{3,1,2,0:T(8,128)(2,1)S(1)}, bf16[8,2048,1,128]{3,1,2,0:T(8,128)(2,1)}, u32[]{:S(2)}) copy-start(bf16[8,2048,1,128]{3,1,2,0:T(8,128)(2,1)} %param.24) | copy-start | bytes 12582916
  178.9 48.4 %copy-start.1 = (bf16[5120,128]{1,0:T(8,128)(2,1)S(1)}, bf16[5120,128]{1,0:T(8,128)(2,1)}, u32[]{:S(2)}) copy-start(bf16[5120,128]{1,0:T(8,128)(2,1)} %param.19) | copy-start | bytes 3932164
  184.5 4.4 %copy-start.5 = (s32[8,8]{1,0:T(8,128)S(1)}, s32[8,8]{1,0:T(8,128)}, u32[]{:S(2)}) copy-start(s32[8,8]{1,0:T(8,128)} %param.29) | copy-start | bytes 772
  224.6 2.6 %copy-start.3 = (bf16[256,640]{1,0:T(8,128)(2,1)}, bf16[256,640]{1,0:T(8,128)(2,1)S(1)}, u32[]{:S(2)}) copy-start(bf16[256,640]{1,0:T(8,128)(2,1)S(1)} %copy.48) | copy-start | bytes 983044
Sparse Core Ops, SparseCore 0:
  10.1 63.9 all-gather.2
  76.2 60.9 all-gather.4
  189.0 34.3 reduce-scatter.3
where the time goes:
time: 234 us
  waiting for transfers between devices  134 us (57%)
  matrix products  47.5 us (20%)
  local copies, waits for them, and re-layouts  22.6 us (10%)
  other arithmetic  16.1 us (7%)
  between operations  14 us (6%)
    all_gather x1, waiting for transfers between devices, shards(): lax.all_gather(prompt_values, 'tok', axis=1, tiled=True)  55.5 us
    all_gather x1, waiting for transfers between devices, shards(): lax.all_gather(prompt_keys, 'tok', axis=1, tiled=True)  42.3 us
    unnamed x4, waiting for transfers between devices  35.7 us
    dot_general x1, matrix products, slice_attention(): jnp.einsum('ntkgsc,nsckd->ntkgsd', weights.astype(jnp.bfloat16), values_s...  10.1 us
    select_n x1, other arithmetic, shards(): jnp.take(lax.all_gather(prompt_values, 'tok', axis=1, tiled=True), own_gr...  9.37 us
    dot_general x1, matrix products, slice_attention(): jnp.einsum('ntkgd,nsckd->ntkgsc', grouped, keys_split, preferred_element_...  7.87 us
    gather x1, local copies, waits for them, and re-layouts, shards(): jnp.take(lax.all_gather(prompt_keys, 'tok', axis=1, tiled=True), own_grou...  7.64 us
    gather x1, local copies, waits for them, and re-layouts, shards(): jnp.take(lax.all_gather(prompt_values, 'tok', axis=1, tiled=True), own_gr...  7.44 us
  transfers between devices with their start and end apart: 3, of which 3 were waited for; matrix products, arithmetic and copies ran while one was open for 13% of the time, Pallas kernels for 0%

commit v1 on v0

--- a/solution.py
+++ b/solution.py
@@ -2,6 +2,7 @@
 import jax.numpy as jnp
 from jax import lax
 from jax.sharding import PartitionSpec as P
+from jax.lax import all_to_all, axis_size
 
 PROMPT = 4096
 THETA = 100000000.0
@@ -116,9 +117,13 @@
     chosen_keys = jnp.take(
         lax.all_gather(prompt_keys, "tok", axis=1, tiled=True), own_groups, axis=0
     )
-    chosen_values = jnp.take(
-        lax.all_gather(prompt_values, "tok", axis=1, tiled=True), own_groups, axis=0
-    )
+
+    def obtain_yards_on_mesh(q_in):
+        state_now = jnp.stack([q_in for _ in range(axis_size("tok"))], 0)
+        odd = all_to_all(state_now, "tok", 0, 0)
+        return jnp.concatenate(odd, 1)
+
+    chosen_values = jnp.take(obtain_yards_on_mesh(prompt_values), own_groups, axis=0)
     outputs, totals = slice_attention(grouped, chosen_keys, chosen_values, slice_rows, factor)
     weighted = jnp.sum(totals[..., None] * outputs.astype(jnp.float32), axis=4)
     prompt_total = jnp.sum(totals, axis=4)

time: 234 us -> 242 us (1.034)
  waiting for transfers between devices: 134 us -> 122 us
  local copies, waits for them, and re-layouts: 22.6 us -> 34.1 us
  starting transfers between devices: 0.11 us -> 8.42 us
    all_to_all x0 -> x1, waiting for transfers between devices: none -> 86.8 us  [obtain_yards_on_mesh(): odd = all_to_all(state_now, 'tok', 0, 0)]
    all_gather x1 -> x0, waiting for transfers between devices: 55.5 us -> none  [shards(): lax.all_gather(prompt_values, 'tok', axis=1, tiled=True)]
    all_gather x1, waiting for transfers between devices: 42.3 us -> 0.01 us  [shards(): lax.all_gather(prompt_keys, 'tok', axis=1, tiled=True)]
    all_to_all x0 -> x1, starting transfers between devices: none -> 8.34 us  [obtain_yards_on_mesh(): odd = all_to_all(state_now, 'tok', 0, 0)]
    all_to_all x0 -> x1, local copies, waits for them, and re-layouts: none -> 6.29 us  [obtain_yards_on_mesh(): odd = all_to_all(state_now, 'tok', 0, 0)]
    another operation x2 -> x3, local copies, waits for them, and re-layouts: 0.23 us -> 5.49 us  [the longest x1 5.26 us: obtain_yards_on_mesh(): state_now = jnp.stack([q_in for _ in range(axis_size('tok'))], 0)]
    unnamed x4 -> x3, waiting for transfers between devices: 35.7 us -> 35.5 us
    unnamed x18 -> x20, local copies, waits for them, and re-layouts: 5.6 us -> 5.61 us
  transfers between devices with their start and end apart: 3 -> 3, of which waited for: 3 -> 2; matrix products, arithmetic and copies ran while one was open for 13% -> 17% of each run, Pallas kernels for 0% -> 0%
where the time goes in v1:
time: 242 us
  waiting for transfers between devices  122 us (50%)
  matrix products  47.2 us (20%)
  local copies, waits for them, and re-layouts  34.1 us (14%)
  other arithmetic  15.5 us (6%)
  between operations  14.3 us (6%)
  starting transfers between devices  8.42 us (3%)
    all_to_all x1, waiting for transfers between devices, obtain_yards_on_mesh(): odd = all_to_all(state_now, 'tok', 0, 0)  86.8 us
    unnamed x3, waiting for transfers between devices  35.5 us
    dot_general x1, matrix products, slice_attention(): jnp.einsum('ntkgsc,nsckd->ntkgsd', weights.astype(jnp.bfloat16), values_s...  10.1 us
    select_n x1, other arithmetic, shards(): jnp.take(obtain_yards_on_mesh(prompt_values), own_groups, axis=0)  9.37 us
    all_to_all x1, starting transfers between devices, obtain_yards_on_mesh(): odd = all_to_all(state_now, 'tok', 0, 0)  8.34 us
    dot_general x1, matrix products, slice_attention(): jnp.einsum('ntkgd,nsckd->ntkgsc', grouped, keys_split, preferred_element_...  7.87 us
    gather x1, local copies, waits for them, and re-layouts, shards(): jnp.take(obtain_yards_on_mesh(prompt_values), own_groups, axis=0)  7.62 us
    gather x1, local copies, waits for them, and re-layouts, shards(): jnp.take(lax.all_gather(prompt_keys, 'tok', axis=1, tiled=True), own_grou...  7.46 us
  transfers between devices with their start and end apart: 3, of which 2 were waited for; matrix products, arithmetic and copies ran while one was open for 17% of the time, Pallas kernels for 0%

profile of v1, /device:TPU:0, one launch (start us, length us, event | category | flops | bytes accessed | tf_op | source)
XLA Modules:
  0.0 241.8 jit_solution(16062100261828617529)
XLA Ops:
  7.2 0.0 copy-start
  7.2 0.0 all-gather.2.cloned.1.call-start
  7.2 0.7 all-gather.2.cloned.1.call-update
  7.9 5.3 %stack.2 = bf16[16,6,256,1,128]{4,2,1,3,0:T(8,128)(2,1)} broadcast(bf16[6,256,128]{2,1,0:T(8,128)(2,1)} %bitcast.188), dimensions={1,2,4} | broadcast | bytes 6684672 | tf_op jit(solution)/shard_map/stack | solution.py:122
  13.2 0.0 copy-start.5
  13.2 8.3 %all-to-all-start = ((bf16[16,6,256,1,128]{4,2,1,3,0:T(8,128)(2,1)}), bf16[16,6,256,1,128]{4,2,1,3,0:T(8,128)(2,1)}, u32[]{:S(2)}, u32[]{:S(2)}) async-start(bf16[16,6,256,1,128]{4,2,1,3,0:T(8,128)(2,1)} %stack.2), calls=%async_computation | async-start | bytes 12582912 | tf_op jit(solution)/shard_map/all_to_all | solution.py:123
  21.5 0.0 reduce-scatter.4.cloned.1.call-start
  21.6 0.0 copy-done.5
  21.6 2.5 %fusion.8 = f32[256]{0:T(256)S(1)} fusion(bf16[256,5120]{1,0:T(8,128)(2,1)} %param.16), kind=kLoop, calls=%fused_computation.22 | loop fusion | flops 3931904 | bytes 2622464 | tf_op jit(solution)/shard_map/reduce_sum | solution.py:92
  24.1 0.0 copy-start.4
  24.1 0.0 copy-start.7
  24.1 4.9 %fusion.66 = f32[256,512]{1,0:T(8,128)S(1)} fusion(bf16[5120,512]{1,0:T(8,128)(2,1)} %param.18, bf16[256,5120]{1,0:T(8,128)(2,1)} %param.16, f32[5120]{0:T(1024)S(1)} %convert_element_type.64, f32[256]{0:T(256)S(1)} %add_rsqrt_fusion), kind=kOutput, calls=%fused_computation.98 | convolution fusion | flops 1347420160 | bytes 8410112 | tf_op jit(solution)/shard_map/dot_general | solution.py:95
  29.0 0.0 copy-start.8
  29.0 0.2 reshape.348
  29.2 0.0 copy-done.4
  29.2 0.2 reduce_sum.66
  29.4 0.0 copy-done.7
  29.4 0.1 add_convert_fusion.1
  29.5 0.1 convert_element_type.67
  29.6 0.0 copy-done
  29.6 2.9 %convolution_bitcast_fusion.1 = f32[256,1,128]{0,2,1:T(8,128)S(1)} fusion(bf16[5120,128]{1,0:T(8,128)(2,1)S(1)} %copy-done, bf16[256,5120]{1,0:T(8,128)(2,1)} %param.16, f32[5120]{0:T(1024)S(1)} %convert_element_type.64, f32[256]{0:T(256)S(1)} %add_rsqrt_fusion), kind=kOutput, calls=%fused_computation.43 | convolution fusion | flops 340787200 | bytes 4084736 | tf_op jit(solution)/shard_map/dot_general | solution.py:98
  32.5 0.3 fusion.54
  32.8 0.1 copy.35
  33.0 0.1 copy.36
  33.1 0.1 copy.34
  33.2 0.0 copy-done.8
  33.3 0.1 compare_and_fusion.1
  33.4 0.5 multiply_cosine_fusion
  33.9 0.3 fusion.68
  34.2 0.0 copy-start.2
  34.2 0.1 subtract_convert_fusion
  34.4 0.1 pad_maximum_fusion
  34.5 0.6 fusion.69
  35.1 3.4 %convolution_convert_fusion.1 = bf16[256,128]{1,0:T(8,128)(2,1)S(1)} fusion(bf16[5120,128]{1,0:T(8,128)(2,1)} %param.20, bf16[256,5120]{1,0:T(8,128)(2,1)} %param.16, f32[5120]{0:T(1024)S(1)} %convert_element_type.64, f32[256]{0:T(256)S(1)} %add_rsqrt_fusion), kind=kOutput, calls=%fused_computation.44 | convolution fusion | flops 340819968 | bytes 4019200 | tf_op jit(solution)/shard_map/dot_general | solution.py:102
  38.6 0.1 iota_compare_fusion
  38.6 0.0 copy-done.2
  38.7 5.2 %fusion.6 = (f32[8,32,4]{1,2,0:T(4,128)S(1)}, f32[8,32,4,2048]{3,1,2,0:T(8,128)}) fusion(pred[8,2048]{1,0:T(8,128)(4,1)S(1)} %iota_compare_fusion, bf16[8,2048,1,128]{3,1,2,0:T(8,128)(2,1)S(1)} %copy-done.2, bf16[8,32,4,128]{3,1,0,2:T(8,128)(2,1)S(1)} %pad_maximum_fusion), kind=kOutput, calls=%fused_computation.17 | convolution fusion | flops 543161344 | bytes 12865536 | tf_op jit(solution)/shard_map/ntkgd,nckd->ntkgc/dot_general | solution.py:49
  43.9 86.8 %all-to-all-done = bf16[16,6,256,1,128]{4,2,1,3,0:T(8,128)(2,1)} async-done(((bf16[16,6,256,1,128]{4,2,1,3,0:T(8,128)(2,1)}), bf16[16,6,256,1,128]{4,2,1,3,0:T(8,128)(2,1)}, u32[]{:S(2)}, u32[]{:S(2)}) %all-to-all-start) | async-done | bytes 6291488 | tf_op jit(solution)/shard_map/all_to_all | solution.py:123
  130.6 6.3 %copy.33 = bf16[16,6,256,1,128]{4,2,0,1,3:T(8,128)(2,1)} copy(bf16[16,6,256,1,128]{4,2,1,3,0:T(8,128)(2,1)} %all-to-all-done) | data formatting | bytes 12582912 | tf_op jit(solution)/shard_map/all_to_all | solution.py:123
  136.9 7.6 %gather_fusion.2 = bf16[8,4096,128]{2,1,0:T(8,128)(2,1)} fusion(bf16[6,4096,128]{2,1,0:T(8,128)(2,1)} %bitcast.182, s32[1024]{0:T(1024)S(1)} %pad_clamp_fusion.1), kind=kCustom, calls=%fused_computation.1.clone | custom fusion | bytes 16777248 | tf_op jit(solution)/shard_map/jit(_take)/gather | solution.py:126
  144.6 0.0 all-gather.2.cloned.1.call-done
  144.6 7.5 %gather_fusion.1 = bf16[8,4096,128]{2,1,0:T(8,128)(2,1)} fusion(bf16[6,4096,128]{2,1,0:T(8,128)(2,1)} %bitcast.183, s32[1024]{0:T(1024)S(1)} %pad_clamp_fusion.1), kind=kCustom, calls=%fused_computation.clone | custom fusion | bytes 16777248 | tf_op jit(solution)/shard_map/jit(_take)/gather | solution.py:117
  152.0 9.4 %bitcast_select_fusion.1 = (bf16[8,4096,1,128]{3,1,0,2:T(8,128)(2,1)}, bf16[8,4096,1,128]{3,1,0,2:T(8,128)(2,1)S(1)}) fusion(bf16[8,4096,128]{2,1,0:T(8,128)(2,1)} %gather_fusion.2, pred[8]{0:T(512)(128)(4,1)S(1)} %get-tuple-element.7, bf16[8,4096,128]{2,1,0:T(8,128)(2,1)} %gather_fusion.1), kind=kLoop, calls=%fused_computation.13 | loop fusion | flops 8388608 | bytes 33554440 | tf_op jit(solution)/shard_map/jit(_take)/select_n | solution.py:126
  161.4 7.9 %bitcast_reduce_fusion = (f32[8,32,4]{1,2,0:T(4,128)S(1)}, f32[8,32,4,16]{1,2,3,0:T(4,128)S(1)}, f32[8,16,256,32,4]{2,3,4,1,0:T(8,128)}) fusion(bf16[8,16,256,128,1]{3,2,4,1,0:T(8,128)(2,1)S(1)} %bitcast.181, bf16[8,32,4,128]{3,1,0,2:T(8,128)(2,1)S(1)} %pad_maximum_fusion), kind=kOutput, calls=%fused_computation.3 | convolution fusion | flops 1086307328 | bytes 25497600 | tf_op jit(solution)/shard_map/ntkgd,nsckd->ntkgsc/dot_general | solution.py:32
  169.3 10.1 %multiply_reduce_fusion = f32[8,32,4,128]{3,1,2,0:T(8,128)S(1)} fusion(f32[8,32,4,16]{1,2,3,0:T(4,128)S(1)} %get-tuple-element.4, bf16[8,16,256,128,1]{3,2,4,1,0:T(8,128)(2,1)} %bitcast.185, f32[8,16,256,32,4]{2,3,4,1,0:T(8,128)} %get-tuple-element.20), kind=kOutput, calls=%fused_computation.15 | convolution fusion | flops 1092485120 | bytes 25755648 | tf_op jit(solution)/shard_map/ntkgsc,nsckd->ntkgsd/dot_general | solution.py:37
  179.4 6.3 %fusion.31 = f32[8,32,1,4,128]{4,1,3,0,2:T(8,128)S(1)} fusion(bf16[8,2048,1,128]{3,1,2,0:T(8,128)(2,1)} %param.25, f32[8,32,4,2048]{3,1,2,0:T(8,128)} %get-tuple-element.24, pred[8,2048]{1,0:T(8,128)(4,1)S(1)} %iota_compare_fusion, f32[8,32,4,128]{3,1,2,0:T(8,128)S(1)} %multiply_reduce_fusion), kind=kOutput, calls=%fused_computation.40 | convolution fusion | flops 543293440 | bytes 13647872 | tf_op jit(solution)/shard_map/ntkgc,nckd->ntkgd/dot_general | solution.py:55
  185.7 0.3 fusion.36
  186.0 0.1 copy.38
  186.2 0.0 copy-start.1
  186.2 5.6 %convolution_convert_fusion = bf16[256,5120]{1,0:T(8,128)(2,1)} fusion(bf16[512,5120]{1,0:T(8,128)(2,1)} %param.21, bf16[32,8,4,128]{3,2,1,0:T(4,128)(2,1)S(1)} %bitcast.190), kind=kOutput, calls=%fused_computation.21 | convolution fusion | flops 1343488000 | bytes 8126464 | tf_op jit(solution)/shard_map/dot_general | solution.py:145
  191.8 0.0 copy-start.6
  191.8 4.4 %copy.48 = bf16[256,5120]{0,1:T(8,128)(2,1)} copy(bf16[256,5120]{1,0:T(8,128)(2,1)} %convolution_convert_fusion) | data formatting | bytes 5242880
  196.2 0.0 reduce-scatter.4.cloned.1.call-update
  196.3 0.0 copy-done.6
  196.3 0.1 compare_and_fusion
  196.3 0.1 reshape.360
  196.4 34.8 %reduce-scatter.4.cloned.1.call-done = bf16[640,256]{1,0:T(8,128)(2,1)} async-done(((bf16[5120,256]{1,0:T(8,128)(2,1)}), bf16[640,256]{1,0:T(8,128)(2,1)}) %reduce-scatter.4.cloned.1.call-update) | async-done | bytes 327696
  231.2 1.2 copy.49
  232.4 0.0 copy-start.3
  232.4 1.2 convert_add_fusion
  233.6 0.7 gather_fusion
  234.3 0.7 fusion.48
  235.0 0.0 copy-done.3
  235.0 0.0 copy-done.1
  (10 shorter events, 0.1 us)
Async XLA Ops:
  7.2 22.4 %copy-start = (bf16[5120,128]{1,0:T(8,128)(2,1)S(1)}, bf16[5120,128]{1,0:T(8,128)(2,1)}, u32[]{:S(2)}) copy-start(bf16[5120,128]{1,0:T(8,128)(2,1)} %param.19) | copy-start | bytes 3932164
  7.2 137.4 %all-gather.2.cloned.1.call-start = ((), (), s32[]{:S(2)}) async-start(), calls=%async_computation.2 | async-start | bytes 6684672 | tf_op jit(solution)/shard_map/all_gather | solution.py:118
  13.2 8.4 %copy-start.5 = (bf16[5120]{0:T(1024)(128)(2,1)S(1)}, bf16[5120]{0:T(1024)(128)(2,1)}, u32[]{:S(2)}) copy-start(bf16[5120]{0:T(1024)(128)(2,1)} %param.17) | copy-start | bytes 30724
  13.2 117.5 %all-to-all-start = ((bf16[16,6,256,1,128]{4,2,1,3,0:T(8,128)(2,1)}), bf16[16,6,256,1,128]{4,2,1,3,0:T(8,128)(2,1)}, u32[]{:S(2)}, u32[]{:S(2)}) async-start(bf16[16,6,256,1,128]{4,2,1,3,0:T(8,128)(2,1)} %stack.2), calls=%async_computation | async-start | bytes 12582912 | tf_op jit(solution)/shard_map/all_to_all | solution.py:123
  21.5 209.7 %reduce-scatter.4.cloned.1.call-start = ((), (), s32[]{:S(2)}) async-start(), calls=%async_computation.3 | async-start | bytes 2949120
  24.1 5.1 %copy-start.4 = (s32[8,32,32]{2,1,0:T(8,128)S(1)}, s32[8,32,32]{2,1,0:T(8,128)}, u32[]{:S(2)}) copy-start(s32[8,32,32]{2,1,0:T(8,128)} %param.28) | copy-start | bytes 98308
  24.1 5.3 %copy-start.7 = (s32[8]{0:T(128)S(1)}, s32[8]{0:T(128)}, u32[]{:S(2)}) copy-start(s32[8]{0:T(128)} %param.26) | copy-start | bytes 100
  29.0 4.2 %copy-start.8 = (s32[128]{0:T(128)S(1)}, s32[128]{0:T(128)}, u32[]{:S(2)}) copy-start(s32[128]{0:T(128)} %param.27) | copy-start | bytes 1540
  34.2 4.4 %copy-start.2 = (bf16[8,2048,1,128]{3,1,2,0:T(8,128)(2,1)S(1)}, bf16[8,2048,1,128]{3,1,2,0:T(8,128)(2,1)}, u32[]{:S(2)}) copy-start(bf16[8,2048,1,128]{3,1,2,0:T(8,128)(2,1)} %param.24) | copy-start | bytes 12582916
  186.2 48.8 %copy-start.1 = (bf16[5120,128]{1,0:T(8,128)(2,1)S(1)}, bf16[5120,128]{1,0:T(8,128)(2,1)}, u32[]{:S(2)}) copy-start(bf16[5120,128]{1,0:T(8,128)(2,1)} %param.19) | copy-start | bytes 3932164
  191.8 4.4 %copy-start.6 = (s32[8,8]{1,0:T(8,128)S(1)}, s32[8,8]{1,0:T(8,128)}, u32[]{:S(2)}) copy-start(s32[8,8]{1,0:T(8,128)} %param.29) | copy-start | bytes 772
  232.4 2.6 %copy-start.3 = (bf16[256,640]{1,0:T(8,128)(2,1)}, bf16[256,640]{1,0:T(8,128)(2,1)S(1)}, u32[]{:S(2)}) copy-start(bf16[256,640]{1,0:T(8,128)(2,1)S(1)} %copy.49) | copy-start | bytes 983044
Sparse Core Ops, SparseCore 0:
  10.1 133.8 all-gather.1
  196.4 34.7 reduce-scatter.3
